TPU v7x, 32 devices: a whole 2x2x4 slice. The times are simulated.
32 devices in a mesh: dp: 16 (over z, x, core), seq: 2 (over y).
Axes of the slice: x: 2, y: 2, z: 4, core: 2. Of those that a mesh axis runs over, the one named last changes fastest.
Arguments:
- tokens: bfloat16 [16, 512, 1152], P('dp', 'seq'), may hold values from -6 to 6
- segment_ids: int32 [16, 512], P('dp'), may hold values from 0 to 3, never falling along the last dimension, each value on 1 to 256 neighbouring positions
- cotangent: bfloat16 [16, 512, 1152], P('dp', 'seq'), may hold values from -6 to 6
- query_weight: bfloat16 [1152, 1024], P(('dp', 'seq')), may hold values from -0.1875 to 0.1875
- key_weight: bfloat16 [1152, 256], P(('dp', 'seq')), may hold values from -0.1875 to 0.1875
- value_weight: bfloat16 [1152, 256], P(('dp', 'seq')), may hold values from -0.1875 to 0.1875
- output_weight: bfloat16 [1024, 1152], P(('dp', 'seq')), may hold values from -0.1875 to 0.1875
- gate_weight: bfloat16 [1152, 6912], P(('dp', 'seq')), may hold values from -0.1875 to 0.1875
- up_weight: bfloat16 [1152, 6912], P(('dp', 'seq')), may hold values from -0.1875 to 0.1875
- down_weight: bfloat16 [6912, 1152], P(('dp', 'seq')), may hold values from -0.078125 to 0.078125
- input_gain: bfloat16 [1152], P(('dp', 'seq')), may hold values from 0.25 to 1.75
- query_gain: bfloat16 [256], P(('dp', 'seq')), may hold values from 0.25 to 1.75
- key_gain: bfloat16 [256], P(('dp', 'seq')), may hold values from 0.25 to 1.75
- attnout_gain: bfloat16 [1152], P(('dp', 'seq')), may hold values from 0.25 to 1.75
- ffnin_gain: bfloat16 [1152], P(('dp', 'seq')), may hold values from 0.25 to 1.75
- ffnout_gain: bfloat16 [1152], P(('dp', 'seq')), may hold values from 0.25 to 1.75
Outputs:
- output: bfloat16 [16, 512, 1152], P('dp', 'seq')
- input_grad: float32 [16, 512, 1152], P('dp', 'seq')
- grad_query: float32 [1152, 1024], P(('dp', 'seq'))
- grad_key: float32 [1152, 256], P(('dp', 'seq'))
- grad_value: float32 [1152, 256], P(('dp', 'seq'))
- grad_output: float32 [1024, 1152], P(('dp', 'seq'))
- grad_gate: float32 [1152, 6912], P(('dp', 'seq'))
- grad_up: float32 [1152, 6912], P(('dp', 'seq'))
- grad_down: float32 [6912, 1152], P(('dp', 'seq'))
- grad_input_gain: float32 [1152], P(('dp', 'seq'))
- grad_query_gain: float32 [256], P(('dp', 'seq'))
- grad_key_gain: float32 [256], P(('dp', 'seq'))
- grad_attnout_gain: float32 [1152], P(('dp', 'seq'))
- grad_ffnin_gain: float32 [1152], P(('dp', 'seq'))
- grad_ffnout_gain: float32 [1152], P(('dp', 'seq'))
Inputs may be any that keep to these rules, and one draw needn't show every extreme that they name: `segment_ids`: in each row the ids never fall and every id occurs; each document spans 1 to 256 positions, one exactly 256.
All inputs are finite; a program needn't handle non-finite values.
Results may differ from a plain program's by a relative error of at most 0.019.
Values may be sent and summed in bfloat16 or wider, within the bound.
A program may use at most 448 MiB of HBM per device.

v0:
```python
import jax
import jax.numpy as jnp
from jax import lax
from jax.sharding import Mesh
from jax.sharding import PartitionSpec as P

epsilon = 1e-06
rope_base = 1000000.0
masked_score = -1e30


def inverse_rms(values):
    return lax.rsqrt(jnp.mean(values * values, axis=-1, keepdims=True) + epsilon)


def rms_back(grad_normed, normed, inverse):
    return inverse * (grad_normed - normed * jnp.mean(grad_normed * normed, axis=-1, keepdims=True))


def doc_positions(segments):
    length = segments.shape[0]
    smaller = segments[None, :] < segments[:, None]
    starts = jnp.sum(smaller.astype(jnp.int32), axis=1)
    return (jnp.arange(length, dtype=jnp.int32) - starts).astype(jnp.float32)


def rope_tables(positions, head_width):
    half_width = head_width // 2
    frequency = rope_base ** (-(2.0 / head_width) * jnp.arange(half_width, dtype=jnp.float32))
    angles = positions[..., None] * frequency
    return (jnp.cos(angles), jnp.sin(angles))


def rotate(values, cos_table, sin_table):
    half_width = values.shape[-1] // 2
    first_half = values[..., :half_width]
    second_half = values[..., half_width:]
    return jnp.concatenate(
        [
            first_half * cos_table - second_half * sin_table,
            second_half * cos_table + first_half * sin_table,
        ],
        axis=-1,
    )


def matmul(left, right):
    return jnp.dot(left, right, preferred_element_type=jnp.float32)


def contract_rows(left, right):
    return lax.dot_general(
        left, right, (((0,), (0,)), ((), ())), preferred_element_type=jnp.float32
    )


def contract_cols(left, right):
    return lax.dot_general(
        left, right, (((1,), (1,)), ((), ())), preferred_element_type=jnp.float32
    )


def gelu_pair(gate_proj, up_proj):
    return jax.nn.gelu(gate_proj, approximate=True) * up_proj


ALL = ("z", "x", "core", "seq")
PLANE = ("x", "core", "seq")


def exchange(blocks, axes):
    return lax.all_to_all(blocks, axes, split_axis=0, concat_axis=0, tiled=True)


def plane_gather(local):
    return lax.all_gather(local, PLANE, axis=0, tiled=True)


def plane_scatter_sum(partial):
    members = lax.axis_size(PLANE)
    terms = exchange(partial.reshape((members, -1) + partial.shape[1:]), PLANE)
    return jnp.sum(terms.astype(jnp.float32), axis=0)


def body(
    tokens,
    segment_ids,
    cotangent,
    query_weight,
    key_weight,
    value_weight,
    output_weight,
    gate_weight,
    up_weight,
    down_weight,
    input_gain,
    query_gain,
    key_gain,
    attnout_gain,
    ffnin_gain,
    ffnout_gain,
):
    bf16, f32 = (jnp.bfloat16, jnp.float32)
    devices = lax.axis_size(ALL)
    members = lax.axis_size(PLANE)
    planes = lax.axis_size("z")
    seq_count = lax.axis_size("seq")
    width_rows = query_weight.shape[0]
    hidden_rows = down_weight.shape[0]
    head_width = key_weight.shape[1]
    query_width = query_weight.shape[1]
    head_count = query_width // head_width
    qkv_width = query_width + 2 * head_width
    mix_rows = output_weight.shape[0]
    padded = (width_rows + 1 + 7) // 8 * 8
    gains = (input_gain, query_gain, key_gain, attnout_gain, ffnin_gain, ffnout_gain)
    gain_row = jnp.concatenate(gains)
    gain_widths = [g.shape[0] for g in gains]
    gain_row = jnp.pad(gain_row, (0, qkv_width - gain_row.shape[0]))
    qkv_local = jnp.concatenate([query_weight, key_weight, value_weight], axis=1)
    packed = jnp.concatenate([qkv_local, gain_row[None]], axis=0)
    packed = jnp.pad(packed, ((0, padded - width_rows - 1), (0, 0)))
    packed_all = lax.all_gather(packed, ALL, axis=0, tiled=False)
    qkv_full = packed_all[:, :width_rows].reshape(devices * width_rows, qkv_width)
    scales, at = ([], 0)
    for width in gain_widths:
        scales.append(packed_all[:, width_rows, at : at + width].reshape(-1).astype(f32))
        at += width
    input_scale, query_scale, key_scale, attnout_scale, ffnin_scale, ffnout_scale = scales
    output_full = lax.all_gather(output_weight, ALL, axis=0, tiled=True)

    def column_blocks(weight):
        pieces = weight.reshape(width_rows, planes, members, hidden_rows)
        return pieces.transpose(2, 0, 1, 3).reshape(members, width_rows, planes * hidden_rows)

    gate_up = jnp.concatenate([column_blocks(gate_weight), column_blocks(up_weight)], axis=1)
    gate_up = jnp.broadcast_to(gate_up[None], (planes,) + gate_up.shape)
    gate_up = exchange(gate_up.reshape((devices,) + gate_up.shape[2:]), ALL)
    gate_full = gate_up[:, :width_rows].reshape(devices * width_rows, planes * hidden_rows)
    up_full = gate_up[:, width_rows:].reshape(devices * width_rows, planes * hidden_rows)
    down_full = exchange(jnp.broadcast_to(down_weight[None], (planes,) + down_weight.shape), "z")
    down_full = down_full.reshape(planes * hidden_rows, down_weight.shape[1])
    hidden = tokens[0].astype(f32)
    incoming = cotangent[0].astype(f32)
    local_rows = hidden.shape[0]
    full_length = local_rows * seq_count
    offset = lax.axis_index("seq") * local_rows
    segment_row = segment_ids[0]

    def mine(rows):
        return lax.dynamic_slice_in_dim(rows, offset, local_rows)

    my_segments = mine(segment_row)
    cos_full, sin_full = rope_tables(doc_positions(segment_row), head_width)
    cos_table, sin_table = (mine(cos_full), mine(sin_full))
    scale = head_width ** (-0.5)
    row_hidden = lax.all_gather(tokens[0], "seq", axis=0, tiled=True).astype(f32)
    row_normed = (row_hidden * inverse_rms(row_hidden) * input_scale).astype(bf16)
    key_value_raw = matmul(row_normed, qkv_full[:, query_width:])
    row_key_raw = key_value_raw[:, :head_width]
    value_rows = key_value_raw[:, head_width:].astype(bf16)
    key_rows = rotate(
        row_key_raw * inverse_rms(row_key_raw) * key_scale, cos_full, sin_full
    ).astype(bf16)
    inv_input = inverse_rms(hidden)
    norm_input = hidden * inv_input
    normed = (norm_input * input_scale).astype(bf16)
    query_raw = matmul(normed, qkv_full[:, :query_width]).reshape(
        local_rows, head_count, head_width
    )
    inv_query = inverse_rms(query_raw)
    norm_query = query_raw * inv_query
    queries = (
        rotate(norm_query * query_scale, cos_table[:, None, :], sin_table[:, None, :]) * scale
    ).astype(bf16)
    key_raw = mine(row_key_raw)
    inv_key = inverse_rms(key_raw)
    norm_key = key_raw * inv_key
    query_places = offset + jnp.arange(local_rows, dtype=jnp.int32)
    key_places = jnp.arange(full_length, dtype=jnp.int32)
    allowed = (my_segments[:, None] == segment_row[None, :]) & (
        query_places[:, None] >= key_places[None, :]
    )
    raw_scores = jnp.einsum("qhd,kd->hqk", queries, key_rows, preferred_element_type=f32)
    scores = jnp.where(allowed[None], raw_scores, masked_score)
    peak = jnp.max(scores, axis=-1, keepdims=True)
    log_total = peak + jnp.log(jnp.sum(jnp.exp(scores - peak), axis=-1, keepdims=True))
    probs = jnp.exp(scores - log_total)
    probs_low = probs.astype(bf16)
    attn_mix = jnp.einsum("hqk,kd->qhd", probs_low, value_rows, preferred_element_type=f32)
    attn_flat = attn_mix.astype(bf16).reshape(local_rows, query_width)
    attn_raw = matmul(attn_flat, output_full)
    inv_attn = inverse_rms(attn_raw)
    norm_attn = attn_raw * inv_attn
    middle = hidden + norm_attn * attnout_scale
    inv_middle = inverse_rms(middle)
    norm_middle = middle * inv_middle
    ffn_in = (norm_middle * ffnin_scale).astype(bf16)
    plane_in = plane_gather(ffn_in)
    gate_proj = matmul(plane_in, gate_full)
    up_proj = matmul(plane_in, up_full)
    activated, gelu_back = jax.vjp(gelu_pair, gate_proj, up_proj)
    activated_low = activated.astype(bf16)
    ffn_raw = plane_scatter_sum(matmul(activated_low, down_full).astype(bf16))
    inv_ffn = inverse_rms(ffn_raw)
    norm_ffn = ffn_raw * inv_ffn
    result = middle + norm_ffn * ffnout_scale
    ffnout_gain_grad = jnp.sum(incoming * norm_ffn, axis=0)
    ffn_raw_grad = rms_back(incoming * ffnout_scale, norm_ffn, inv_ffn).astype(bf16)
    plane_grad = plane_gather(ffn_raw_grad)
    act_grad = contract_cols(plane_grad, down_full)
    gate_grad, up_grad = gelu_back(act_grad)
    gate_low = gate_grad.astype(bf16)
    up_low = up_grad.astype(bf16)
    ffn_in_grad = plane_scatter_sum(
        (contract_cols(gate_low, gate_full) + contract_cols(up_low, up_full)).astype(bf16)
    )
    down_terms = exchange(
        contract_rows(activated_low, plane_grad)
        .astype(bf16)
        .reshape(planes, hidden_rows, down_weight.shape[1]),
        "z",
    )
    down_wgrad = jnp.sum(down_terms.astype(f32), axis=0)

    def row_blocks(grad):
        return grad.astype(bf16).reshape(devices, width_rows, planes * hidden_rows)

    gate_up_terms = exchange(
        jnp.concatenate(
            [
                row_blocks(contract_rows(plane_in, gate_low)),
                row_blocks(contract_rows(plane_in, up_low)),
            ],
            axis=1,
        ),
        ALL,
    )
    gate_up_sum = jnp.sum(
        gate_up_terms.astype(f32).reshape(planes, members, 2, width_rows, planes, hidden_rows),
        axis=0,
    )
    gate_up_sum = gate_up_sum.transpose(1, 2, 3, 0, 4).reshape(
        2, width_rows, planes * members * hidden_rows
    )
    gate_wgrad, up_wgrad = (gate_up_sum[0], gate_up_sum[1])
    ffnin_gain_grad = jnp.sum(ffn_in_grad * norm_middle, axis=0)
    middle_grad = incoming + rms_back(ffn_in_grad * ffnin_scale, norm_middle, inv_middle)
    attnout_gain_grad = jnp.sum(middle_grad * norm_attn, axis=0)
    attn_raw_grad = rms_back(middle_grad * attnout_scale, norm_attn, inv_attn).astype(bf16)
    output_wgrad = contract_rows(attn_flat, attn_raw_grad)
    mix_grad = (
        contract_cols(attn_raw_grad, output_full)
        .astype(bf16)
        .reshape(local_rows, head_count, head_width)
    )
    prob_grad = jnp.einsum("qhd,kd->hqk", mix_grad, value_rows, preferred_element_type=f32)
    row_delta = jnp.sum(prob_grad * probs, axis=-1, keepdims=True)
    score_grad = (probs * (prob_grad - row_delta)).astype(bf16)
    value_grad_rows = jnp.einsum("hqk,qhd->kd", probs_low, mix_grad, preferred_element_type=f32)
    key_grad_rows = jnp.einsum("hqk,qhd->kd", score_grad, queries, preferred_element_type=f32)
    query_grad = jnp.einsum("hqk,kd->qhd", score_grad, key_rows, preferred_element_type=f32)
    key_value_terms = exchange(
        jnp.concatenate([key_grad_rows, value_grad_rows], axis=1)
        .astype(bf16)
        .reshape(seq_count, local_rows, 2 * head_width),
        "seq",
    )
    key_value_grad = jnp.sum(key_value_terms.astype(f32), axis=0)
    key_grad, value_grad = (key_value_grad[:, :head_width], key_value_grad[:, head_width:])
    query_norm_grad = rotate(query_grad * scale, cos_table[:, None, :], -sin_table[:, None, :])
    query_gain_grad = jnp.sum(query_norm_grad * norm_query, axis=(0, 1))
    query_raw_low = (
        rms_back(query_norm_grad * query_scale, norm_query, inv_query)
        .astype(bf16)
        .reshape(local_rows, query_width)
    )
    key_norm_grad = rotate(key_grad, cos_table, -sin_table)
    key_gain_grad = jnp.sum(key_norm_grad * norm_key, axis=0)
    key_raw_low = rms_back(key_norm_grad * key_scale, norm_key, inv_key).astype(bf16)
    qkv_raw_low = jnp.concatenate([query_raw_low, key_raw_low, value_grad.astype(bf16)], axis=1)
    qkv_wgrad = contract_rows(normed, qkv_raw_low)
    normed_grad = contract_cols(qkv_raw_low, qkv_full)
    input_gain_grad = jnp.sum(normed_grad * norm_input, axis=0)
    input_grad = middle_grad + rms_back(normed_grad * input_scale, norm_input, inv_input)

    def to_owners(grad):
        rows, columns = (grad.shape[0] // devices, grad.shape[1])
        blocks = grad.astype(bf16).reshape(planes, members, rows, columns)
        terms = exchange(blocks.transpose(1, 0, 2, 3), PLANE)
        summed = jnp.sum(terms.astype(f32), axis=0).astype(bf16)
        return jnp.sum(exchange(summed, "z").astype(f32), axis=0)

    output_share = to_owners(output_wgrad)
    gain_grads = (
        input_gain_grad,
        query_gain_grad,
        key_gain_grad,
        attnout_gain_grad,
        ffnin_gain_grad,
        ffnout_gain_grad,
    )
    gain_rows = jnp.concatenate([g.reshape(devices, -1) for g in gain_grads], axis=1)
    gain_rows = jnp.pad(gain_rows, ((0, 0), (0, qkv_width - gain_rows.shape[1])))
    qkv_blocks = jnp.concatenate(
        [qkv_wgrad.reshape(devices, width_rows, qkv_width), gain_rows[:, None]], axis=1
    )
    qkv_blocks = jnp.pad(qkv_blocks, ((0, 0), (0, padded - width_rows - 1), (0, 0)))
    qkv_share = to_owners(qkv_blocks.reshape(devices * padded, qkv_width))
    gain_shares, at = ([], 0)
    for width in gain_widths:
        gain_shares.append(qkv_share[width_rows, at : at + width])
        at += width
    return (
        result.astype(bf16)[None],
        input_grad[None],
        qkv_share[:width_rows, :query_width],
        qkv_share[:width_rows, query_width : query_width + head_width],
        qkv_share[:width_rows, query_width + head_width :],
        output_share,
        gate_wgrad,
        up_wgrad,
        down_wgrad,
        *gain_shares,
    )


def solution(mesh):
    dp, seq = (mesh.shape["dp"], mesh.shape["seq"])
    split = Mesh(mesh.devices.reshape(dp // 4, 2, 2, seq), ALL)
    rows = P(("z", "x", "core"), "seq", None)
    matrix, vector = (P(ALL, None), P(ALL))
    return jax.shard_map(
        body,
        mesh=split,
        in_specs=(rows, P(("z", "x", "core"), None), rows) + (matrix,) * 7 + (vector,) * 6,
        out_specs=(rows, rows) + (matrix,) * 7 + (vector,) * 6,
        check_vma=False,
    )
```

profile of v0, /device:TPU:0, one launch (start us, length us, event | category | flops | bytes accessed | tf_op | source)
XLA Modules:
  0.0 778.4 jit_solution(3174932612226022172)
XLA Ops:
  22.3 7.4 all-to-all-start
  31.6 18.9 %all-gather.14.cloned.1.call-done = bf16[1,512,1152]{2,1,0:T(8,128)(2,1)} async-done(((bf16[1,256,1152]{2,1,0:T(8,128)(2,1)}), bf16[1,512,1152]{2,1,0:T(8,128)(2,1)}) %all-gather.14.cloned.1.call-update) | async-done | bytes 1179664 | tf_op jit(solution)/shard_map/all_gather | solution.py:157
  52.1 88.6 %all-gather.16.cloned.1.call-done = bf16[1280,1536]{1,0:T(8,128)(2,1)} async-done(((bf16[40,1536]{1,0:T(8,128)(2,1)}), bf16[1280,1536]{1,0:T(8,128)(2,1)}) %all-gather.16.cloned.1.call-update) | async-done | bytes 3932176 | tf_op jit(solution)/shard_map/all_gather | solution.py:123
  141.7 5.7 reshape.363
  175.6 24.2 %all-gather.8.cloned.1.call-done = bf16[1024,1152]{1,0:T(8,128)(2,1)} async-done(((bf16[32,1152]{1,0:T(8,128)(2,1)}), bf16[1024,1152]{1,0:T(8,128)(2,1)}) %all-gather.8.cloned.1.call-update) | async-done | bytes 2359312 | tf_op jit(solution)/shard_map/all_gather | solution.py:130
  210.0 5.0 all-to-all-start.1
  215.0 5.4 fusion.100
  228.7 16.8 %all-gather.10.cloned.1.call-done = bf16[2048,1152]{1,0:T(8,128)(2,1)} async-done(((bf16[256,1152]{1,0:T(8,128)(2,1)}), bf16[2048,1152]{1,0:T(8,128)(2,1)}) %all-gather.10.cloned.1.call-update) | async-done | bytes 4718608 | tf_op jit(solution)/shard_map/all_gather | solution.py:76
  245.5 7.6 fusion.106
  256.1 9.3 %multiply_convert_fusion.1 = (bf16[2048,864]{0,1:T(8,128)(2,1)}, f32[2048,864]{0,1:T(8,128)}) fusion(f32[2048,864]{0,1:T(8,128)S(1)} %fusion.106, bf16[2048,1152]{1,0:T(8,128)(2,1)S(1)} %copy-done.59, bf16[1152,864]{1,0:T(8,128)(2,1)S(1)} %copy-done.22), kind=kOutput, calls=%fused_computation.17 | convolution fusion | flops 4094558208 | bytes 24403968 | tf_op jit(solution)/shard_map/dot_general | solution.py:48
  265.3 9.2 %convolution_convert_fusion = bf16[2048,1152]{1,0:T(8,128)(2,1)} fusion(bf16[2048,864]{0,1:T(8,128)(2,1)} %get-tuple-element.75, bf16[864,1152]{1,0:T(8,128)(2,1)} %bitcast.18), kind=kOutput, calls=%fused_computation.8 | convolution fusion | flops 4079222784 | bytes 10248192 | tf_op jit(solution)/shard_map/dot_general | solution.py:48
  274.6 4.6 all-to-all-start.2
  280.8 52.2 %all-to-all-done.2 = bf16[8,256,1152]{2,1,0:T(8,128)(2,1)} async-done(((bf16[8,256,1152]{2,1,0:T(8,128)(2,1)}), bf16[8,256,1152]{2,1,0:T(8,128)(2,1)}, u32[]{:S(2)}, u32[]{:S(2)}) %all-to-all-start.2) | async-done | bytes 4718624 | tf_op jit(solution)/shard_map/all_to_all | solution.py:72
  338.9 39.1 %all-gather.12.cloned.1.call-done = bf16[2048,1152]{1,0:T(8,128)(2,1)} async-done(((bf16[256,1152]{1,0:T(8,128)(2,1)}), bf16[2048,1152]{1,0:T(8,128)(2,1)}) %all-gather.12.cloned.1.call-update) | async-done | bytes 4718608 | tf_op jit(solution)/shard_map/all_gather | solution.py:76
  378.0 14.8 %multiply_convert_fusion = (bf16[2048,864]{0,1:T(8,128)(2,1)S(1)}, bf16[2048,864]{0,1:T(8,128)(2,1)S(1)}) fusion(f32[2048,864]{0,1:T(8,128)} %copy-done.60, f32[2048,864]{0,1:T(8,128)} %get-tuple-element.76, bf16[2048,1152]{1,0:T(8,128)(2,1)} %all-gather.12.cloned.1.call-done, bf16[864,1152]{1,0:T(8,128)(2,1)} %bitcast.18), kind=kOutput, calls=%fused_computation.16 | convolution fusion | flops 4119330816 | bytes 27942912 | tf_op jit(solution)/shard_map/dot_general | solution.py:58
  392.8 5.8 fusion.107
  398.6 7.7 add_convert_fusion
  406.3 4.6 all-to-all-start.3
  413.8 51.0 %all-to-all-done.3 = bf16[8,256,1152]{2,1,0:T(8,128)(2,1)} async-done(((bf16[8,256,1152]{2,1,0:T(8,128)(2,1)}), bf16[8,256,1152]{2,1,0:T(8,128)(2,1)}, u32[]{:S(2)}, u32[]{:S(2)}) %all-to-all-start.3) | async-done | bytes 4718624 | tf_op jit(solution)/shard_map/all_to_all | solution.py:72
  487.7 5.9 all-to-all-done.4
  500.9 9.5 %convolution_convert_fusion.5 = bf16[864,1152]{1,0:T(8,128)(2,1)} fusion(bf16[2048,864]{0,1:T(8,128)(2,1)} %get-tuple-element.75, bf16[2048,1152]{1,0:T(8,128)(2,1)} %all-gather.12.cloned.1.call-done), kind=kOutput, calls=%fused_computation.27 | convolution fusion | flops 4077858816 | bytes 10248192 | tf_op jit(solution)/shard_map/dot_general | solution.py:52
  512.0 15.0 %all-to-all-done.7 = bf16[8,4,32,1152]{3,2,1,0:T(8,128)(2,1)S(1)} async-done(((bf16[8,4,32,1152]{3,2,1,0:T(8,128)(2,1)}), bf16[8,4,32,1152]{3,2,1,0:T(8,128)(2,1)S(1)}, u32[]{:S(2)}, u32[]{:S(2)}) %all-to-all-start.7) | async-done | bytes 2359328 | tf_op jit(solution)/shard_map/all_to_all | solution.py:72
  526.9 4.6 all-to-all-start.10
  568.2 9.6 %all-to-all-done.10 = bf16[4,216,1152]{2,1,0:T(8,128)(2,1)} async-done(((bf16[4,216,1152]{2,1,0:T(8,128)(2,1)}), bf16[4,216,1152]{2,1,0:T(8,128)(2,1)}, u32[]{:S(2)}, u32[]{:S(2)}) %all-to-all-start.10) | async-done | bytes 1990688 | tf_op jit(solution)/shard_map/all_to_all | solution.py:72
  590.3 4.7 all-to-all-start.5
  595.0 8.1 %convolution_convert_fusion.3 = bf16[1152,864]{0,1:T(8,128)(2,1)S(1)} fusion(bf16[2048,864]{0,1:T(8,128)(2,1)} %copy-done.62, bf16[2048,1152]{1,0:T(8,128)(2,1)} %all-gather.10.cloned.1.call-done), kind=kOutput, calls=%fused_computation.25 | convolution fusion | flops 4077858816 | bytes 10248192 | tf_op jit(solution)/shard_map/dot_general | solution.py:52
  608.2 9.4 %convolution_convert_fusion.4 = bf16[1152,864]{0,1:T(8,128)(2,1)} fusion(bf16[2048,864]{0,1:T(8,128)(2,1)} %copy-done.61, bf16[2048,1152]{1,0:T(8,128)(2,1)} %all-gather.10.cloned.1.call-done), kind=kOutput, calls=%fused_computation.26 | convolution fusion | flops 4077858816 | bytes 10248192 | tf_op jit(solution)/shard_map/dot_general | solution.py:52
  625.6 4.8 pad_maximum_fusion
  630.4 10.1 %all-to-all-done.5 = bf16[8,4,40,1536]{3,2,1,0:T(8,128)(2,1)} async-done(((bf16[8,4,40,1536]{3,2,1,0:T(8,128)(2,1)}), bf16[8,4,40,1536]{3,2,1,0:T(8,128)(2,1)}, u32[]{:S(2)}, u32[]{:S(2)}) %all-to-all-start.5) | async-done | bytes 3932192 | tf_op jit(solution)/shard_map/all_to_all | solution.py:72
  650.7 86.4 %all-to-all-done.9 = bf16[32,72,864]{2,1,0:T(8,128)(2,1)} async-done(((bf16[32,72,864]{2,1,0:T(8,128)(2,1)}), bf16[32,72,864]{2,1,0:T(8,128)(2,1)}, u32[]{:S(2)}, u32[]{:S(2)}) %all-to-all-start.9) | async-done | bytes 3981344 | tf_op jit(solution)/shard_map/all_to_all | solution.py:72
  743.5 12.2 %reshape.397 = f32[4,8,2,36,4,216]{5,4,3,2,1,0:T(4,128)} reshape(bf16[32,72,864]{2,1,0:T(8,128)(2,1)} %all-to-all-done.9) | data formatting | bytes 11943936 | tf_op jit(solution)/shard_map/reshape | solution.py:240
  755.7 7.0 reduce_sum.324
  (290 shorter events, 198.3 us)
Async XLA Ops:
  7.2 10.1 %copy-start.28 = (bf16[36,6912]{1,0:T(8,128)(2,1)S(1)}, bf16[36,6912]{1,0:T(8,128)(2,1)}, u32[]{:S(2)}) copy-start(bf16[36,6912]{1,0:T(8,128)(2,1)} %param.23) | copy-start | bytes 1492996
  7.2 43.3 %all-gather.14.cloned.1.call-start = ((), (), s32[]{:S(2)}) async-start(), calls=%async_computation.14 | async-start | bytes 1769472 | tf_op jit(solution)/shard_map/all_gather | solution.py:157
  7.9 132.8 %all-gather.16.cloned.1.call-start = ((), (), s32[]{:S(2)}) async-start(), calls=%async_computation.15 | async-start | bytes 4055040 | tf_op jit(solution)/shard_map/all_gather | solution.py:123
  22.3 185.2 %all-to-all-start = ((bf16[32,72,864]{2,1,0:T(8,128)(2,1)}), bf16[32,72,864]{2,1,0:T(8,128)(2,1)}, u32[]{:S(2)}, u32[]{:S(2)}) async-start(bf16[32,72,864]{2,1,0:T(8,128)(2,1)} %bitcast.214), calls=%async_computation | async-start | bytes 8257536 | tf_op jit(solution)/shard_map/all_to_all | solution.py:72
  29.7 170.1 %all-gather.8.cloned.1.call-start = ((), (), s32[]{:S(2)}) async-start(), calls=%async_computation.11 | async-start | bytes 2433024 | tf_op jit(solution)/shard_map/all_gather | solution.py:130
  30.5 215.0 %all-gather.10.cloned.1.call-start = ((), (), s32[]{:S(2)}) async-start(), calls=%async_computation.12 | async-start | bytes 5308416 | tf_op jit(solution)/shard_map/all_gather | solution.py:76
  31.1 123.2 %copy-start.54 = (f32[256]{0:T(256)}, f32[256]{0:T(256)S(1)}, u32[]{:S(2)}) copy-start(f32[256]{0:T(256)S(1)} %add_rsqrt_fusion.7) | copy-start | bytes 3076
  31.1 116.3 %copy-start.56 = (s32[1,256]{1,0:T(1,128)}, s32[1,256]{1,0:T(1,128)S(1)}, u32[]{:S(2)}) copy-start(s32[1,256]{1,0:T(1,128)S(1)} %constant_dynamic-slice_fusion.2) | copy-start | bytes 3076
  161.1 13.0 %copy-start.18 = (f32[512,512]{0,1:T(8,128)}, f32[512,512]{0,1:T(8,128)S(1)}, u32[]{:S(2)}) copy-start(f32[512,512]{0,1:T(8,128)S(1)} %fusion.46) | copy-start | bytes 3145732
  174.1 29.4 %copy-start.40 = (f32[4,256]{1,0:T(4,128)}, f32[4,256]{1,0:T(4,128)S(1)}, u32[]{:S(2)}) copy-start(f32[4,256]{1,0:T(4,128)S(1)} %log_add_fusion) | copy-start | bytes 12292
  175.6 28.5 %copy-start.39 = (f32[32,36]{1,0:T(8,128)S(1)}, f32[32,36]{1,0:T(8,128)}, u32[]{:S(2)}) copy-start(f32[32,36]{1,0:T(8,128)} %get-tuple-element.16) | copy-start | bytes 13828
  210.0 55.3 %all-to-all-start.1 = ((bf16[4,216,1152]{2,1,0:T(8,128)(2,1)}), bf16[4,216,1152]{2,1,0:T(8,128)(2,1)}, u32[]{:S(2)}, u32[]{:S(2)}) async-start(bf16[4,216,1152]{2,1,0:T(8,128)(2,1)} %broadcast_in_dim.29), calls=%async_computation.1 | async-start | bytes 3981312 | tf_op jit(solution)/shard_map/all_to_all | solution.py:72
  245.5 10.6 %copy-start.22 = (bf16[1152,864]{1,0:T(8,128)(2,1)S(1)}, bf16[1152,864]{1,0:T(8,128)(2,1)}, u32[]{:S(2)}) copy-start(bf16[1152,864]{1,0:T(8,128)(2,1)} %reshape.371) | copy-start | bytes 5971972
  245.5 10.6 %copy-start.59 = (bf16[2048,1152]{1,0:T(8,128)(2,1)S(1)}, bf16[2048,1152]{1,0:T(8,128)(2,1)}, u32[]{:S(2)}) copy-start(bf16[2048,1152]{1,0:T(8,128)(2,1)} %all-gather.10.cloned.1.call-done) | copy-start | bytes 14155780
  274.6 58.5 %all-to-all-start.2 = ((bf16[8,256,1152]{2,1,0:T(8,128)(2,1)}), bf16[8,256,1152]{2,1,0:T(8,128)(2,1)}, u32[]{:S(2)}, u32[]{:S(2)}) async-start(bf16[8,256,1152]{2,1,0:T(8,128)(2,1)} %bitcast.221), calls=%async_computation.2 | async-start | bytes 9437184 | tf_op jit(solution)/shard_map/all_to_all | solution.py:72
  279.2 98.8 %all-gather.12.cloned.1.call-start = ((), (), s32[]{:S(2)}) async-start(), calls=%async_computation.13 | async-start | bytes 5308416 | tf_op jit(solution)/shard_map/all_gather | solution.py:76
  378.0 14.8 %copy-start.21 = (bf16[1152,864]{1,0:T(8,128)(2,1)S(1)}, bf16[1152,864]{1,0:T(8,128)(2,1)}, u32[]{:S(2)}) copy-start(bf16[1152,864]{1,0:T(8,128)(2,1)} %reshape.370) | copy-start | bytes 5971972
  406.3 58.5 %all-to-all-start.3 = ((bf16[8,256,1152]{2,1,0:T(8,128)(2,1)}), bf16[8,256,1152]{2,1,0:T(8,128)(2,1)}, u32[]{:S(2)}, u32[]{:S(2)}) async-start(bf16[8,256,1152]{2,1,0:T(8,128)(2,1)} %bitcast.220), calls=%async_computation.3 | async-start | bytes 9437184 | tf_op jit(solution)/shard_map/all_to_all | solution.py:72
  481.7 11.9 %all-to-all-start.4 = ((bf16[2,256,512]{1,2,0:T(8,128)(2,1)}), bf16[2,256,512]{1,2,0:T(8,128)(2,1)S(1)}, u32[]{:S(2)}, u32[]{:S(2)}) async-start(bf16[2,256,512]{1,2,0:T(8,128)(2,1)} %pad_maximum_fusion.4), calls=%async_computation.4 | async-start | bytes 1048576 | tf_op jit(solution)/shard_map/all_to_all | solution.py:72
  494.4 32.5 %all-to-all-start.7 = ((bf16[8,4,32,1152]{3,2,1,0:T(8,128)(2,1)}), bf16[8,4,32,1152]{3,2,1,0:T(8,128)(2,1)S(1)}, u32[]{:S(2)}, u32[]{:S(2)}) async-start(bf16[8,4,32,1152]{3,2,1,0:T(8,128)(2,1)} %bitcast.217), calls=%async_computation.7 | async-start | bytes 4718592 | tf_op jit(solution)/shard_map/all_to_all | solution.py:72
  500.9 9.6 %copy-start.14 = (bf16[4,256,512]{1,2,0:T(8,128)(2,1)S(1)}, bf16[4,256,512]{1,2,0:T(8,128)(2,1)}, u32[]{:S(2)}) copy-start(bf16[4,256,512]{1,2,0:T(8,128)(2,1)} %copy-done.13) | copy-start | bytes 3145732
  500.9 9.6 %copy-start.30 = (bf16[512,128]{0,1:T(8,128)(2,1)S(1)}, bf16[512,128]{0,1:T(8,128)(2,1)}, u32[]{:S(2)}) copy-start(bf16[512,128]{0,1:T(8,128)(2,1)} %get-tuple-element.67) | copy-start | bytes 393220
  526.9 50.8 %all-to-all-start.10 = ((bf16[4,216,1152]{2,1,0:T(8,128)(2,1)}), bf16[4,216,1152]{2,1,0:T(8,128)(2,1)}, u32[]{:S(2)}, u32[]{:S(2)}) async-start(bf16[4,216,1152]{2,1,0:T(8,128)(2,1)} %bitcast.232), calls=%async_computation.10 | async-start | bytes 3981312 | tf_op jit(solution)/shard_map/all_to_all | solution.py:72
  541.3 10.7 %copy-start.16 = (f32[512,256]{0,1:T(8,128)S(1)}, f32[512,256]{0,1:T(8,128)}, u32[]{:S(2)}) copy-start(f32[512,256]{0,1:T(8,128)} %get-tuple-element.48) | copy-start | bytes 1572868
  541.3 10.7 %copy-start.47 = (f32[256]{0:T(256)S(1)}, f32[256]{0:T(256)}, u32[]{:S(2)}) copy-start(f32[256]{0:T(256)} %copy-done.46) | copy-start | bytes 3076
  541.3 10.7 %copy-start.57 = (f32[256]{0:T(256)S(1)}, f32[256]{0:T(256)}, u32[]{:S(2)}) copy-start(f32[256]{0:T(256)} %add_rsqrt_fusion.3) | copy-start | bytes 3076
  577.8 12.5 %all-to-all-start.8 = ((bf16[4,32,1152]{2,1,0:T(8,128)(2,1)}), bf16[4,32,1152]{2,1,0:T(8,128)(2,1)S(1)}, u32[]{:S(2)}, u32[]{:S(2)}) async-start(bf16[4,32,1152]{2,1,0:T(8,128)(2,1)} %reduce_sum.322), calls=%async_computation.8 | async-start | bytes 589824 | tf_op jit(solution)/shard_map/all_to_all | solution.py:72
  590.3 50.2 %all-to-all-start.5 = ((bf16[8,4,40,1536]{3,2,1,0:T(8,128)(2,1)}), bf16[8,4,40,1536]{3,2,1,0:T(8,128)(2,1)}, u32[]{:S(2)}, u32[]{:S(2)}) async-start(bf16[8,4,40,1536]{3,2,1,0:T(8,128)(2,1)} %bitcast.215), calls=%async_computation.5 | async-start | bytes 7864320 | tf_op jit(solution)/shard_map/all_to_all | solution.py:72
  640.5 96.6 %all-to-all-start.9 = ((bf16[32,72,864]{2,1,0:T(8,128)(2,1)}), bf16[32,72,864]{2,1,0:T(8,128)(2,1)}, u32[]{:S(2)}, u32[]{:S(2)}) async-start(bf16[32,72,864]{2,1,0:T(8,128)(2,1)} %pad_maximum_fusion), calls=%async_computation.9 | async-start | bytes 8257536 | tf_op jit(solution)/shard_map/all_to_all | solution.py:72
  647.0 94.5 %copy-start.4 = (f32[256,1152]{1,0:T(8,128)S(1)}, f32[256,1152]{1,0:T(8,128)}, u32[]{:S(2)}) copy-start(f32[256,1152]{1,0:T(8,128)} %copy-done.3) | copy-start | bytes 3538948
  647.0 94.5 %copy-start.10 = (f32[256,1152]{1,0:T(8,128)S(1)}, f32[256,1152]{1,0:T(8,128)}, u32[]{:S(2)}) copy-start(f32[256,1152]{1,0:T(8,128)} %copy-done.9) | copy-start | bytes 3538948
  737.1 31.0 %all-to-all-start.6 = ((bf16[4,40,1536]{2,1,0:T(8,128)(2,1)}), bf16[4,40,1536]{2,1,0:T(8,128)(2,1)}, u32[]{:S(2)}, u32[]{:S(2)}) async-start(bf16[4,40,1536]{2,1,0:T(8,128)(2,1)} %reduce_sum.320), calls=%async_computation.6 | async-start | bytes 983040 | tf_op jit(solution)/shard_map/all_to_all | solution.py:72
  (47 other events, 161.5 us)
Sparse Core Ops, SparseCore 0:
  9.6 40.9 all-gather.13
  54.0 86.6 all-gather.15
  143.6 56.1 all-gather.7
  207.7 37.7 all-gather.9
  339.0 38.8 all-gather.11
where the time goes:
time: 785 us; the launch traced here: 778 us
  waiting for transfers between devices  423 us (54%)
  local copies, waits for them, and re-layouts  114 us (15%)
  matrix products  108 us (14%)
  other arithmetic  67.4 us (9%)
  starting transfers between devices  50.4 us (6%)
  between operations  15.1 us (2%)
    all_to_all x11, waiting for transfers between devices, exchange(): return lax.all_to_all(blocks, axes, split_axis=0, concat_axis=0, tiled=True)  234 us
    all_gather x1, waiting for transfers between devices, body(): packed_all = lax.all_gather(packed, ALL, axis=0, tiled=False)  88.6 us
    all_gather x2, waiting for transfers between devices, plane_gather(): return lax.all_gather(local, PLANE, axis=0, tiled=True)  55.9 us
    all_to_all x11, starting transfers between devices, exchange(): return lax.all_to_all(blocks, axes, split_axis=0, concat_axis=0, tiled=True)  49.7 us
    dot_general x6, matrix products, matmul(): return jnp.dot(left, right, preferred_element_type=jnp.float32)  35.1 us
    dot_general x5, matrix products, contract_cols(): lax.dot_general(left, right, (((1,), (1,)), ((), ())), preferred_element_...  32.7 us
    dot_general x5, matrix products, contract_rows(): lax.dot_general(left, right, (((0,), (0,)), ((), ())), preferred_element_...  32.2 us
    all_gather x1, waiting for transfers between devices, body(): output_full = lax.all_gather(output_weight, ALL, axis=0, tiled=True)  24.2 us
  transfers between devices with their start and end apart: 16, of which 13 were waited for; matrix products, arithmetic and copies ran while one was open for 28% of the time, Pallas kernels for 0%

commit v1 on v0

--- a/solution.py
+++ b/solution.py
@@ -7,6 +7,18 @@
 epsilon = 1e-06
 rope_base = 1000000.0
 masked_score = -1e30
+
+
+def doubled_up(array, axis, dim):
+    ways, here, step = (lax.axis_size(axis), lax.axis_index(axis), array.shape[dim])
+    line, have = (array, 1)
+    while have < ways:
+        line = jnp.concatenate(
+            [line, lax.ppermute(line, axis, [(d, (d - have) % ways) for d in range(ways)])],
+            axis=dim,
+        )
+        have = 2 * have
+    return jnp.roll(line, here * step, axis=dim)
 
 
 def inverse_rms(values):
@@ -154,7 +166,7 @@
     cos_full, sin_full = rope_tables(doc_positions(segment_row), head_width)
     cos_table, sin_table = (mine(cos_full), mine(sin_full))
     scale = head_width ** (-0.5)
-    row_hidden = lax.all_gather(tokens[0], "seq", axis=0, tiled=True).astype(f32)
+    row_hidden = doubled_up(tokens[0], "seq", 0).astype(f32)
     row_normed = (row_hidden * inverse_rms(row_hidden) * input_scale).astype(bf16)
     key_value_raw = matmul(row_normed, qkv_full[:, query_width:])
     row_key_raw = key_value_raw[:, :head_width]

time: 785 us -> 755 us (0.962)
  waiting for transfers between devices: 423 us -> 382 us
    all_gather x1, waiting for transfers between devices: 88.6 us -> 69.4 us  [body(): packed_all = lax.all_gather(packed, ALL, axis=0, tiled=False)]
    all_gather x1 -> x0, waiting for transfers between devices: 18.9 us -> none  [body(): lax.all_gather(tokens[0], 'seq', axis=0, tiled=True).astype(f32)]
  transfers between devices with their start and end apart: 16 -> 16, of which waited for: 13 -> 12; matrix products, arithmetic and copies ran while one was open for 28% -> 30% of each run, Pallas kernels for 0% -> 0%
where the time goes in v1:
time: 755 us; the launch traced here: 748 us
  waiting for transfers between devices  382 us (51%)
  local copies, waits for them, and re-layouts  120 us (16%)
  matrix products  108 us (14%)
  other arithmetic  71.1 us (9%)
  starting transfers between devices  51 us (7%)
  between operations  15.1 us (2%)
    all_to_all x11, waiting for transfers between devices, exchange(): return lax.all_to_all(blocks, axes, split_axis=0, concat_axis=0, tiled=True)  233 us
    all_gather x1, waiting for transfers between devices, body(): packed_all = lax.all_gather(packed, ALL, axis=0, tiled=False)  69.4 us
    all_gather x2, waiting for transfers between devices, plane_gather(): return lax.all_gather(local, PLANE, axis=0, tiled=True)  56.1 us
    all_to_all x11, starting transfers between devices, exchange(): return lax.all_to_all(blocks, axes, split_axis=0, concat_axis=0, tiled=True)  47.1 us
    dot_general x5, matrix products, contract_cols(): lax.dot_general(left, right, (((1,), (1,)), ((), ())), preferred_element_...  34.7 us
    dot_general x6, matrix products, matmul(): return jnp.dot(left, right, preferred_element_type=jnp.float32)  34.7 us
    dot_general x5, matrix products, contract_rows(): lax.dot_general(left, right, (((0,), (0,)), ((), ())), preferred_element_...  32 us
    all_gather x1, waiting for transfers between devices, body(): output_full = lax.all_gather(output_weight, ALL, axis=0, tiled=True)  22.3 us
  transfers between devices with their start and end apart: 16, of which 12 were waited for; matrix products, arithmetic and copies ran while one was open for 30% of the time, Pallas kernels for 0%

profile of v1, /device:TPU:0, one launch (start us, length us, event | category | flops | bytes accessed | tf_op | source)
XLA Modules:
  0.0 747.7 jit_solution(5580783710138876210)
XLA Ops:
  24.7 5.0 all-to-all-start
  36.2 69.4 %all-gather.12.cloned.1.call-done = bf16[1280,1536]{1,0:T(8,128)(2,1)} async-done(((bf16[40,1536]{1,0:T(8,128)(2,1)}), bf16[1280,1536]{1,0:T(8,128)(2,1)}) %all-gather.12.cloned.1.call-update) | async-done | bytes 3932176 | tf_op jit(solution)/shard_map/all_gather | solution.py:135
  146.2 22.3 %all-gather.6.cloned.1.call-done = bf16[1024,1152]{1,0:T(8,128)(2,1)} async-done(((bf16[32,1152]{1,0:T(8,128)(2,1)}), bf16[1024,1152]{1,0:T(8,128)(2,1)}) %all-gather.6.cloned.1.call-update) | async-done | bytes 2359312 | tf_op jit(solution)/shard_map/all_gather | solution.py:142
  177.5 4.6 all-to-all-start.1
  182.1 5.5 fusion.97
  195.9 17.1 %all-gather.8.cloned.1.call-done = bf16[2048,1152]{1,0:T(8,128)(2,1)} async-done(((bf16[256,1152]{1,0:T(8,128)(2,1)}), bf16[2048,1152]{1,0:T(8,128)(2,1)}) %all-gather.8.cloned.1.call-update) | async-done | bytes 4718608 | tf_op jit(solution)/shard_map/all_gather | solution.py:88
  212.9 7.6 %fusion.103 = f32[2048,864]{0,1:T(8,128)S(1)} fusion(bf16[2048,1152]{1,0:T(8,128)(2,1)} %all-gather.8.cloned.1.call-done, bf16[1152,864]{1,0:T(8,128)(2,1)} %reshape.370), kind=kOutput, calls=%fused_computation.224 | convolution fusion | flops 4076863488 | bytes 13787136 | tf_op jit(solution)/shard_map/dot_general | solution.py:60
  223.5 9.2 %multiply_convert_fusion.1 = (bf16[2048,864]{0,1:T(8,128)(2,1)}, f32[2048,864]{0,1:T(8,128)}) fusion(f32[2048,864]{0,1:T(8,128)S(1)} %fusion.103, bf16[2048,1152]{1,0:T(8,128)(2,1)S(1)} %copy-done.60, bf16[1152,864]{1,0:T(8,128)(2,1)S(1)} %copy-done.26), kind=kOutput, calls=%fused_computation.17 | convolution fusion | flops 4094558208 | bytes 24403968 | tf_op jit(solution)/shard_map/dot_general | solution.py:60
  232.7 9.2 %convolution_convert_fusion = bf16[2048,1152]{1,0:T(8,128)(2,1)} fusion(bf16[2048,864]{0,1:T(8,128)(2,1)} %get-tuple-element.78, bf16[864,1152]{1,0:T(8,128)(2,1)} %bitcast.16), kind=kOutput, calls=%fused_computation.8 | convolution fusion | flops 4079222784 | bytes 10248192 | tf_op jit(solution)/shard_map/dot_general | solution.py:60
  241.9 4.7 all-to-all-start.2
  247.1 53.5 %all-to-all-done.2 = bf16[8,256,1152]{2,1,0:T(8,128)(2,1)} async-done(((bf16[8,256,1152]{2,1,0:T(8,128)(2,1)}), bf16[8,256,1152]{2,1,0:T(8,128)(2,1)}, u32[]{:S(2)}, u32[]{:S(2)}) %all-to-all-start.2) | async-done | bytes 4718624 | tf_op jit(solution)/shard_map/all_to_all | solution.py:84
  306.4 39.1 %all-gather.10.cloned.1.call-done = bf16[2048,1152]{1,0:T(8,128)(2,1)} async-done(((bf16[256,1152]{1,0:T(8,128)(2,1)}), bf16[2048,1152]{1,0:T(8,128)(2,1)}) %all-gather.10.cloned.1.call-update) | async-done | bytes 4718608 | tf_op jit(solution)/shard_map/all_gather | solution.py:88
  345.5 14.8 %multiply_convert_fusion = (bf16[2048,864]{0,1:T(8,128)(2,1)S(1)}, bf16[2048,864]{0,1:T(8,128)(2,1)S(1)}) fusion(f32[2048,864]{0,1:T(8,128)} %copy-done.61, f32[2048,864]{0,1:T(8,128)} %get-tuple-element.79, bf16[2048,1152]{1,0:T(8,128)(2,1)} %all-gather.10.cloned.1.call-done, bf16[864,1152]{1,0:T(8,128)(2,1)} %bitcast.16), kind=kOutput, calls=%fused_computation.16 | convolution fusion | flops 4119330816 | bytes 27942912 | tf_op jit(solution)/shard_map/dot_general | solution.py:70
  360.3 5.8 fusion.104
  366.1 7.9 %add_convert_fusion = bf16[2048,1152]{1,0:T(8,128)(2,1)} fusion(f32[2048,1152]{1,0:T(8,128)S(1)} %fusion.104, bf16[2048,864]{0,1:T(8,128)(2,1)S(1)} %get-tuple-element.38, bf16[1152,864]{1,0:T(8,128)(2,1)S(1)} %copy-done.27), kind=kOutput, calls=%fused_computation.3 | convolution fusion | flops 4081582080 | bytes 19685376 | tf_op jit(solution)/shard_map/dot_general | solution.py:70
  374.0 4.7 all-to-all-start.3
  381.9 50.8 %all-to-all-done.3 = bf16[8,256,1152]{2,1,0:T(8,128)(2,1)} async-done(((bf16[8,256,1152]{2,1,0:T(8,128)(2,1)}), bf16[8,256,1152]{2,1,0:T(8,128)(2,1)}, u32[]{:S(2)}, u32[]{:S(2)}) %all-to-all-start.3) | async-done | bytes 4718624 | tf_op jit(solution)/shard_map/all_to_all | solution.py:84
  455.5 5.9 all-to-all-done.4
  468.0 9.5 %convolution_convert_fusion.5 = bf16[864,1152]{1,0:T(8,128)(2,1)} fusion(bf16[2048,864]{0,1:T(8,128)(2,1)} %get-tuple-element.78, bf16[2048,1152]{1,0:T(8,128)(2,1)} %all-gather.10.cloned.1.call-done), kind=kOutput, calls=%fused_computation.27 | convolution fusion | flops 4077858816 | bytes 10248192 | tf_op jit(solution)/shard_map/dot_general | solution.py:64
  485.7 8.8 %all-to-all-done.7 = bf16[8,4,32,1152]{3,2,1,0:T(8,128)(2,1)S(1)} async-done(((bf16[8,4,32,1152]{3,2,1,0:T(8,128)(2,1)}), bf16[8,4,32,1152]{3,2,1,0:T(8,128)(2,1)S(1)}, u32[]{:S(2)}, u32[]{:S(2)}) %all-to-all-start.7) | async-done | bytes 2359328 | tf_op jit(solution)/shard_map/all_to_all | solution.py:84
  494.5 4.6 all-to-all-start.10
  513.7 5.4 fusion.38
  534.5 10.9 %all-to-all-done.10 = bf16[4,216,1152]{2,1,0:T(8,128)(2,1)} async-done(((bf16[4,216,1152]{2,1,0:T(8,128)(2,1)}), bf16[4,216,1152]{2,1,0:T(8,128)(2,1)}, u32[]{:S(2)}, u32[]{:S(2)}) %all-to-all-start.10) | async-done | bytes 1990688 | tf_op jit(solution)/shard_map/all_to_all | solution.py:84
  557.9 4.7 all-to-all-start.5
  562.7 8.1 %convolution_convert_fusion.3 = bf16[1152,864]{0,1:T(8,128)(2,1)S(1)} fusion(bf16[2048,864]{0,1:T(8,128)(2,1)} %copy-done.63, bf16[2048,1152]{1,0:T(8,128)(2,1)} %all-gather.8.cloned.1.call-done), kind=kOutput, calls=%fused_computation.25 | convolution fusion | flops 4077858816 | bytes 10248192 | tf_op jit(solution)/shard_map/dot_general | solution.py:64
  575.8 9.4 %convolution_convert_fusion.4 = bf16[1152,864]{0,1:T(8,128)(2,1)} fusion(bf16[2048,864]{0,1:T(8,128)(2,1)} %copy-done.62, bf16[2048,1152]{1,0:T(8,128)(2,1)} %all-gather.8.cloned.1.call-done), kind=kOutput, calls=%fused_computation.26 | convolution fusion | flops 4077858816 | bytes 10248192 | tf_op jit(solution)/shard_map/dot_general | solution.py:64
  593.3 4.8 pad_maximum_fusion
  598.1 10.1 %all-to-all-done.5 = bf16[8,4,40,1536]{3,2,1,0:T(8,128)(2,1)} async-done(((bf16[8,4,40,1536]{3,2,1,0:T(8,128)(2,1)}), bf16[8,4,40,1536]{3,2,1,0:T(8,128)(2,1)}, u32[]{:S(2)}, u32[]{:S(2)}) %all-to-all-start.5) | async-done | bytes 3932192 | tf_op jit(solution)/shard_map/all_to_all | solution.py:84
  615.3 89.4 %all-to-all-done.9 = bf16[32,72,864]{2,1,0:T(8,128)(2,1)} async-done(((bf16[32,72,864]{2,1,0:T(8,128)(2,1)}), bf16[32,72,864]{2,1,0:T(8,128)(2,1)}, u32[]{:S(2)}, u32[]{:S(2)}) %all-to-all-start.9) | async-done | bytes 3981344 | tf_op jit(solution)/shard_map/all_to_all | solution.py:84
  704.7 4.4 all-to-all-start.6
  712.7 12.2 %reshape.397 = f32[4,8,2,36,4,216]{5,4,3,2,1,0:T(4,128)} reshape(bf16[32,72,864]{2,1,0:T(8,128)(2,1)} %all-to-all-done.9) | data formatting | bytes 11943936 | tf_op jit(solution)/shard_map/reshape | solution.py:252
  724.9 7.0 reduce_sum.324
  (290 shorter events, 206.2 us)
Async XLA Ops:
  7.2 12.5 %copy-start.33 = (bf16[36,6912]{1,0:T(8,128)(2,1)S(1)}, bf16[36,6912]{1,0:T(8,128)(2,1)}, u32[]{:S(2)}) copy-start(bf16[36,6912]{1,0:T(8,128)(2,1)} %param.23) | copy-start | bytes 1492996
  7.2 98.4 %all-gather.12.cloned.1.call-start = ((), (), s32[]{:S(2)}) async-start(), calls=%async_computation.14 | async-start | bytes 4055040 | tf_op jit(solution)/shard_map/all_gather | solution.py:135
  13.0 20.4 %collective-permute-start = (bf16[256,1152]{1,0:T(8,128)(2,1)}, bf16[256,1152]{1,0:T(8,128)(2,1)S(1)}, u32[]{:S(2)}, u32[]{:S(2)}) collective-permute-start(bf16[256,1152]{1,0:T(8,128)(2,1)} %bitcast.185), channel_id=1, source_target_pairs={{0,1},{1,0},{2,3},{3,2},{4,5},{5,4},{6,7},{7,6},{8,9},{9,8},{10,11... | collective-permute-start | bytes 1769480 | tf_op jit(solution)/shard_map/ppermute | solution.py:17
  24.7 150.3 %all-to-all-start = ((bf16[32,72,864]{2,1,0:T(8,128)(2,1)}), bf16[32,72,864]{2,1,0:T(8,128)(2,1)}, u32[]{:S(2)}, u32[]{:S(2)}) async-start(bf16[32,72,864]{2,1,0:T(8,128)(2,1)} %bitcast.180), calls=%async_computation | async-start | bytes 8257536 | tf_op jit(solution)/shard_map/all_to_all | solution.py:84
  29.7 138.8 %all-gather.6.cloned.1.call-start = ((), (), s32[]{:S(2)}) async-start(), calls=%async_computation.11 | async-start | bytes 2433024 | tf_op jit(solution)/shard_map/all_gather | solution.py:142
  30.4 182.5 %all-gather.8.cloned.1.call-start = ((), (), s32[]{:S(2)}) async-start(), calls=%async_computation.12 | async-start | bytes 5308416 | tf_op jit(solution)/shard_map/all_gather | solution.py:88
  31.2 76.0 %copy-start.55 = (s32[256]{0:T(256)}, s32[256]{0:T(256)S(1)}, u32[]{:S(2)}) copy-start(s32[256]{0:T(256)S(1)} %iota_add_fusion) | copy-start | bytes 3076
  31.3 93.1 %copy-start.57 = (f32[256]{0:T(256)}, f32[256]{0:T(256)S(1)}, u32[]{:S(2)}) copy-start(f32[256]{0:T(256)S(1)} %add_rsqrt_fusion.7) | copy-start | bytes 3076
  31.3 75.9 %copy-start.52 = (s32[1,256]{1,0:T(1,128)}, s32[1,256]{1,0:T(1,128)S(1)}, u32[]{:S(2)}) copy-start(s32[1,256]{1,0:T(1,128)S(1)} %constant_dynamic-slice_fusion.2) | copy-start | bytes 3076
  111.1 23.9 %copy-start.3 = (bf16[1152,1536]{1,0:T(8,128)(2,1)}, bf16[1152,1536]{1,0:T(8,128)(2,1)S(1)}, u32[]{:S(2)}) copy-start(bf16[1152,1536]{1,0:T(8,128)(2,1)S(1)} %reshape.363) | copy-start | bytes 10616836
  146.2 26.0 %copy-start.18 = (bf16[256,4,256]{2,0,1:T(8,128)(2,1)}, bf16[256,4,256]{2,0,1:T(8,128)(2,1)S(1)}, u32[]{:S(2)}) copy-start(bf16[256,4,256]{2,0,1:T(8,128)(2,1)S(1)} %convolution_convert_fusion.7) | copy-start | bytes 1572868
  146.2 25.9 %copy-start.44 = (f32[32,36]{1,0:T(8,128)S(1)}, f32[32,36]{1,0:T(8,128)}, u32[]{:S(2)}) copy-start(f32[32,36]{1,0:T(8,128)} %get-tuple-element.16) | copy-start | bytes 13828
  177.5 55.2 %all-to-all-start.1 = ((bf16[4,216,1152]{2,1,0:T(8,128)(2,1)}), bf16[4,216,1152]{2,1,0:T(8,128)(2,1)}, u32[]{:S(2)}, u32[]{:S(2)}) async-start(bf16[4,216,1152]{2,1,0:T(8,128)(2,1)} %broadcast_in_dim.29), calls=%async_computation.1 | async-start | bytes 3981312 | tf_op jit(solution)/shard_map/all_to_all | solution.py:84
  212.9 10.6 %copy-start.26 = (bf16[1152,864]{1,0:T(8,128)(2,1)S(1)}, bf16[1152,864]{1,0:T(8,128)(2,1)}, u32[]{:S(2)}) copy-start(bf16[1152,864]{1,0:T(8,128)(2,1)} %reshape.371) | copy-start | bytes 5971972
  212.9 10.6 %copy-start.60 = (bf16[2048,1152]{1,0:T(8,128)(2,1)S(1)}, bf16[2048,1152]{1,0:T(8,128)(2,1)}, u32[]{:S(2)}) copy-start(bf16[2048,1152]{1,0:T(8,128)(2,1)} %all-gather.8.cloned.1.call-done) | copy-start | bytes 14155780
  241.9 58.6 %all-to-all-start.2 = ((bf16[8,256,1152]{2,1,0:T(8,128)(2,1)}), bf16[8,256,1152]{2,1,0:T(8,128)(2,1)}, u32[]{:S(2)}, u32[]{:S(2)}) async-start(bf16[8,256,1152]{2,1,0:T(8,128)(2,1)} %bitcast.189), calls=%async_computation.2 | async-start | bytes 9437184 | tf_op jit(solution)/shard_map/all_to_all | solution.py:84
  246.7 98.8 %all-gather.10.cloned.1.call-start = ((), (), s32[]{:S(2)}) async-start(), calls=%async_computation.13 | async-start | bytes 5308416 | tf_op jit(solution)/shard_map/all_gather | solution.py:88
  345.5 14.8 %copy-start.25 = (bf16[1152,864]{1,0:T(8,128)(2,1)S(1)}, bf16[1152,864]{1,0:T(8,128)(2,1)}, u32[]{:S(2)}) copy-start(bf16[1152,864]{1,0:T(8,128)(2,1)} %reshape.370) | copy-start | bytes 5971972
  374.0 58.6 %all-to-all-start.3 = ((bf16[8,256,1152]{2,1,0:T(8,128)(2,1)}), bf16[8,256,1152]{2,1,0:T(8,128)(2,1)}, u32[]{:S(2)}, u32[]{:S(2)}) async-start(bf16[8,256,1152]{2,1,0:T(8,128)(2,1)} %bitcast.188), calls=%async_computation.3 | async-start | bytes 9437184 | tf_op jit(solution)/shard_map/all_to_all | solution.py:84
  449.5 11.9 %all-to-all-start.4 = ((bf16[2,256,512]{1,2,0:T(8,128)(2,1)}), bf16[2,256,512]{1,2,0:T(8,128)(2,1)S(1)}, u32[]{:S(2)}, u32[]{:S(2)}) async-start(bf16[2,256,512]{1,2,0:T(8,128)(2,1)} %pad_maximum_fusion.4), calls=%async_computation.4 | async-start | bytes 1048576 | tf_op jit(solution)/shard_map/all_to_all | solution.py:84
  462.2 32.3 %all-to-all-start.7 = ((bf16[8,4,32,1152]{3,2,1,0:T(8,128)(2,1)}), bf16[8,4,32,1152]{3,2,1,0:T(8,128)(2,1)S(1)}, u32[]{:S(2)}, u32[]{:S(2)}) async-start(bf16[8,4,32,1152]{3,2,1,0:T(8,128)(2,1)} %bitcast.183), calls=%async_computation.7 | async-start | bytes 4718592 | tf_op jit(solution)/shard_map/all_to_all | solution.py:84
  468.0 9.6 %copy-start.39 = (bf16[512,128]{0,1:T(8,128)(2,1)S(1)}, bf16[512,128]{0,1:T(8,128)(2,1)}, u32[]{:S(2)}) copy-start(bf16[512,128]{0,1:T(8,128)(2,1)} %copy-done.38) | copy-start | bytes 393220
  494.5 50.9 %all-to-all-start.10 = ((bf16[4,216,1152]{2,1,0:T(8,128)(2,1)}), bf16[4,216,1152]{2,1,0:T(8,128)(2,1)}, u32[]{:S(2)}, u32[]{:S(2)}) async-start(bf16[4,216,1152]{2,1,0:T(8,128)(2,1)} %bitcast.200), calls=%async_computation.10 | async-start | bytes 3981312 | tf_op jit(solution)/shard_map/all_to_all | solution.py:84
  499.1 11.3 %copy-start.22 = (f32[256,128]{0,1:T(8,128)S(1)}, f32[256,128]{0,1:T(8,128)}, u32[]{:S(2)}) copy-start(f32[256,128]{0,1:T(8,128)} %copy-done.21) | copy-start | bytes 393220
  501.4 10.0 %copy-start.14 = (f32[512,256]{0,1:T(8,128)S(1)}, f32[512,256]{0,1:T(8,128)}, u32[]{:S(2)}) copy-start(f32[512,256]{0,1:T(8,128)} %get-tuple-element.50) | copy-start | bytes 1572868
  501.4 10.0 %copy-start.48 = (f32[256]{0:T(256)S(1)}, f32[256]{0:T(256)}, u32[]{:S(2)}) copy-start(f32[256]{0:T(256)} %reshape.390) | copy-start | bytes 3076
  503.5 10.2 %copy-start.46 = (f32[1152]{0:T(1024)S(1)}, f32[1152]{0:T(1024)}, u32[]{:S(2)}) copy-start(f32[1152]{0:T(1024)} %reshape.389) | copy-start | bytes 13828
  533.4 15.5 %copy-start.32 = (bf16[32,1,1536]{2,1,0:T(2,128)(2,1)S(1)}, bf16[32,1,1536]{2,1,0:T(2,128)(2,1)}, u32[]{:S(2)}) copy-start(bf16[32,1,1536]{2,1,0:T(2,128)(2,1)} %copy.193) | copy-start | bytes 294916
  545.4 12.5 %all-to-all-start.8 = ((bf16[4,32,1152]{2,1,0:T(8,128)(2,1)}), bf16[4,32,1152]{2,1,0:T(8,128)(2,1)S(1)}, u32[]{:S(2)}, u32[]{:S(2)}) async-start(bf16[4,32,1152]{2,1,0:T(8,128)(2,1)} %reduce_sum.322), calls=%async_computation.8 | async-start | bytes 589824 | tf_op jit(solution)/shard_map/all_to_all | solution.py:84
  557.9 50.2 %all-to-all-start.5 = ((bf16[8,4,40,1536]{3,2,1,0:T(8,128)(2,1)}), bf16[8,4,40,1536]{3,2,1,0:T(8,128)(2,1)}, u32[]{:S(2)}, u32[]{:S(2)}) async-start(bf16[8,4,40,1536]{3,2,1,0:T(8,128)(2,1)} %bitcast.181), calls=%async_computation.5 | async-start | bytes 7864320 | tf_op jit(solution)/shard_map/all_to_all | solution.py:84
  608.1 96.6 %all-to-all-start.9 = ((bf16[32,72,864]{2,1,0:T(8,128)(2,1)}), bf16[32,72,864]{2,1,0:T(8,128)(2,1)}, u32[]{:S(2)}, u32[]{:S(2)}) async-start(bf16[32,72,864]{2,1,0:T(8,128)(2,1)} %pad_maximum_fusion), calls=%async_computation.9 | async-start | bytes 8257536 | tf_op jit(solution)/shard_map/all_to_all | solution.py:84
  704.7 32.5 %all-to-all-start.6 = ((bf16[4,40,1536]{2,1,0:T(8,128)(2,1)}), bf16[4,40,1536]{2,1,0:T(8,128)(2,1)}, u32[]{:S(2)}, u32[]{:S(2)}) async-start(bf16[4,40,1536]{2,1,0:T(8,128)(2,1)} %reduce_sum.320), calls=%async_computation.6 | async-start | bytes 983040 | tf_op jit(solution)/shard_map/all_to_all | solution.py:84
  (48 other events, 163.1 us)
Sparse Core Ops, SparseCore 0:
  13.1 92.3 all-gather.11
  108.5 59.9 all-gather.5
  175.1 37.7 all-gather.7
  306.5 38.8 all-gather.9
